TPU v7x, 32 devices: a whole 2x2x4 slice. The times are simulated.
32 devices in a mesh: section: 4 (over x, core), expert: 8 (over z, y).
Axes of the slice: x: 2, y: 2, z: 4, core: 2. Of those that a mesh axis runs over, the one named last changes fastest.
Arguments:
- sent_acts: bfloat16 [4, 512, 2048], P('section', 'expert'), may hold values from -6 to 6
- stash: bfloat16 [4, 512, 2048], P('section', 'expert'), may hold values from -6 to 6
- cotangents: bfloat16 [4, 512, 2048], P('section', 'expert'), may hold values from -6 to 6
- norm_gain: bfloat16 [4, 2048], P('section'), may hold values from 0.5 to 1.5
- w_gate: bfloat16 [4, 16, 2048, 768], P('section', 'expert'), may hold values from -0.125 to 0.125
- w_up: bfloat16 [4, 16, 2048, 768], P('section', 'expert'), may hold values from -0.125 to 0.125
- w_down: bfloat16 [4, 16, 768, 2048], P('section', 'expert'), may hold values from -0.21875 to 0.21875
- routes_next: int32 [4, 512, 8], P('section', 'expert'), may hold values from 0 to 15, all different within a row; in each aligned block of 64 rows (0 to 63, 64 to 127, ..., all dimensions but the last counted through in order) at most 48 rows name the same one
- gates_next: bfloat16 [4, 512, 8], P('section', 'expert'), may hold values from 0.049804688 to 0.5
- routes_prev: int32 [4, 512, 8], P('section', 'expert'), may hold values from 0 to 15, all different within a row; in each aligned block of 64 rows (0 to 63, 64 to 127, ..., all dimensions but the last counted through in order) at most 48 rows name the same one
- gates_prev: bfloat16 [4, 512, 8], P('section', 'expert'), may hold values from 0.049804688 to 0.5
Outputs:
- fwd_out: bfloat16 [4, 512, 2048], P('section', 'expert')
- bwd_out: bfloat16 [4, 512, 2048], P('section', 'expert')
- gate_grad: bfloat16 [4, 512, 8], P('section', 'expert')
- grad_w_gate: bfloat16 [4, 16, 2048, 768], P('section', 'expert')
- grad_w_up: bfloat16 [4, 16, 2048, 768], P('section', 'expert')
- grad_w_down: bfloat16 [4, 16, 768, 2048], P('section', 'expert')
Inputs may be any that keep to these rules, and one draw needn't show every extreme that they name: `routes_next`: each row names 8 different experts. At most 48 of the 64 tokens of one device choose one expert, and in some device's tokens some expert is chosen by exactly 48. `routes_prev`: each row names 8 different experts. At most 48 of the 64 tokens of one device choose one expert, and in some device's tokens some expert is chosen by exactly 48.
All inputs are finite; a program needn't handle non-finite values.
Results may differ from a plain program's by a relative error of at most 0.008.
Values may be sent and summed in bfloat16 or wider, within the bound.
A program may use at most 128 MiB of HBM per device.

v0:
```python
import functools

import jax
import jax.numpy as jnp
from jax import lax
from jax.experimental import pallas as pl
from jax.experimental.pallas import tpu as pltpu
from jax.sharding import PartitionSpec as P

EPS = 1e-06
F32 = jnp.float32
BF16 = jnp.bfloat16
LANES = 128
VMEM = pl.BlockSpec(memory_space=pltpu.VMEM)


class Ring:
    def __init__(self, sections, owners):
        bits = owners.bit_length() - 1
        self.n = owners
        self.half = owners // 2
        self.nz = 1 << ((bits + 1) // 2)
        self.ny = owners // self.nz
        self.section = lax.axis_index("section")
        self.sections = sections
        self.me = lax.axis_index("expert")
        z, y = self.me // self.ny, self.me % self.ny
        self.place = y * self.nz + z + (y % 2) * (self.nz - 1 - 2 * z)
        self.sides = (self.owner(1), self.owner(-1))

    def owner(self, offset):
        p = (self.place + offset + self.n) % self.n
        y, r = p // self.nz, p % self.nz
        return (r + (y % 2) * (self.nz - 1 - 2 * r)) * self.ny + y

    def peer(self, offset):
        return (self.me + offset) % self.n

    def device(self, expert):
        return (self.section, expert)

    def shifted(self, by):
        return ((self.section + by + self.sections) % self.sections, self.me)

    def greet(self, sections_too):
        barrier = pltpu.get_barrier_semaphore()
        targets = [self.device(self.peer(r)) for r in range(1, self.n)]
        if sections_too:
            targets += [self.shifted(1), self.shifted(-1)]
        for target in targets:
            pl.semaphore_signal(
                barrier, inc=1, device_id=target, device_id_type=pl.DeviceIdType.MESH
            )
        pl.semaphore_wait(barrier, len(targets))


def send(src, dst, send_sem, recv_sem, device):
    return pltpu.make_async_remote_copy(
        src_ref=src,
        dst_ref=dst,
        send_sem=send_sem,
        recv_sem=recv_sem,
        device_id=device,
        device_id_type=pl.DeviceIdType.MESH,
    )


def normed(rows, gain):
    values = rows.astype(F32)
    scale = lax.rsqrt(jnp.mean(values * values, axis=-1, keepdims=True) + EPS)
    return (values * scale * gain).astype(BF16)


def dot(a, b, ca, cb):
    return lax.dot_general(a, b, (((ca,), (cb,)), ((), ())), preferred_element_type=F32)


def flat(ref):
    value = ref[...]
    return value.reshape(-1, value.shape[-1])


def tile_of(size):
    return 256 if size % 256 == 0 else LANES


def columns(i, tile):
    return pl.ds(pl.multiple_of(i * tile, tile), tile)


def gate_column(gates_ref, index):
    rows = flat(gates_ref).astype(F32)
    lane = lax.broadcasted_iota(jnp.int32, rows.shape, 1)
    return jnp.sum(jnp.where(lane == index, rows, 0.0), axis=1, keepdims=True)


def load_weights(hbm, held, sems):
    copies = [pltpu.make_async_copy(h, v, sems.at[i]) for i, (h, v) in enumerate(zip(hbm, held))]
    for copy in copies:
        copy.start()
    return copies


def gather_kernel(
    sections, owners,
    act_ref, stash_ref, cot_ref, gain_ref, dense_ref, wg_hbm, wu_hbm, wd_hbm,
    arrived_ref, next_ref, prev_ref, cots_ref, gates_ref,
    d_gate_ref, d_up_ref, gated_ref, row_ref, products_ref,
    wg, wu, wd, pre_gate, pre_up, sums,
    shift_send, shift_recv, gate_send, gate_recv, ring_send, ring_recv, weight_sem,
):
    ring = Ring(sections, owners)
    me, half = ring.me, ring.half
    tokens, width = stash_ref.shape
    local, _, units = wg.shape
    cut = width // 2
    loads = load_weights((wg_hbm, wu_hbm, wd_hbm), (wg, wu, wd), weight_sem)
    ring.greet(True)
    cot_shift = send(cot_ref, cots_ref.at[me], shift_send.at[0], shift_recv.at[0], ring.shifted(-1))
    act_shift = send(act_ref, arrived_ref, shift_send.at[1], shift_recv.at[1], ring.shifted(1))
    cot_shift.start()
    act_shift.start()
    prev_ref[me] = normed(stash_ref[...], gain_ref[...])
    gates_ref[me] = dense_ref[...]
    buffers = (prev_ref, cots_ref, next_ref)
    flying = {}

    def start(t, k):
        made = []
        for d, way in enumerate((1, -1)):
            block = ring.owner(-way * k)
            ref = buffers[t].at[block]
            if k == half - 1:
                ref = ref.at[:, pl.ds(d * cut, cut)]
            made.append(
                send(ref, ref, ring_send.at[t, d, k], ring_recv.at[t, d, k], ring.device(ring.sides[d]))
            )
        flying[t, k] = made
        for copy in made:
            copy.start()

    def arrive(t, k):
        for copy in flying[t, k]:
            copy.wait_recv()

    def advance(t, k):
        if k < half:
            arrive(t, k - 1)
            start(t, k)

    tile = tile_of(units)

    def pre_activations(j):
        @pl.loop(0, units // tile)
        def _(i):
            cols = columns(i, tile)
            rows = flat(prev_ref)
            pre_gate[j, :, cols] = dot(rows, wg[j, :, cols], 1, 0)
            pre_up[j, :, cols] = dot(rows, wu[j, :, cols], 1, 0)

    def gradients(j):
        weight = gate_column(gates_ref, (owners + me) * local + j)
        sums[j] = jnp.zeros(sums.shape[1:], F32)

        @pl.loop(0, units // tile)
        def _(i):
            cols = columns(i, tile)
            plain = dot(flat(cots_ref), wd[j, cols, :], 1, 1)
            gate, up = pre_gate[j, :, cols], pre_up[j, :, cols]
            sigma = jax.nn.sigmoid(gate)
            active = gate * sigma
            hidden = active * up
            d_hidden = weight * plain
            sums[j] += jnp.sum(hidden * plain, axis=1, keepdims=True)
            gated_ref[j, :, cols] = (weight * hidden).astype(BF16)
            d_gate_ref[j, :, cols] = (d_hidden * up * sigma * (1.0 + gate * (1.0 - sigma))).astype(BF16)
            d_up_ref[j, :, cols] = (d_hidden * active).astype(BF16)

    wide = tile_of(width)

    def row_gradients(low, high):
        @pl.loop(low, high)
        def _(i):
            cols = columns(i, wide)
            total = 0.0
            for j in range(local):
                total = total + dot(d_gate_ref[j], wg[j, cols, :], 1, 1)
                total = total + dot(d_up_ref[j], wu[j, cols, :], 1, 1)
            row_ref[:, :, cols] = total.astype(BF16).reshape(owners, tokens, wide)

    start(0, 0)
    gate_copies = [
        send(dense_ref, gates_ref.at[me], gate_send.at[r - 1], gate_recv.at[r - 1], ring.device(ring.peer(r)))
        for r in range(1, owners)
    ]
    for copy in gate_copies:
        copy.start()
    cot_shift.wait()
    start(1, 0)
    act_shift.wait()
    next_ref[me] = normed(arrived_ref[...], gain_ref[...])
    for k in range(1, half):
        advance(0, k)
        if k >= 2:
            advance(1, k - 1)
    start(2, 0)
    for copy in loads:
        copy.wait()
    for copy in gate_copies:
        copy.wait()
    arrive(0, half - 1)
    pre_activations(0)
    advance(1, half - 1)
    for j in range(1, local):
        pre_activations(j)
    advance(2, 1)
    arrive(1, half - 1)
    for j in range(local):
        gradients(j)
        advance(2, 2 + j)
    steps = list(range(2 + local, half))
    row_gradients(0, width // wide // 2)
    for k in steps:
        advance(2, k)
    row_gradients(width // wide // 2, width // wide)
    lane = lax.broadcasted_iota(jnp.int32, sums.shape[1:], 1)
    total = jnp.zeros(sums.shape[1:], F32)
    for j in range(local):
        total = jnp.where(lane == j, sums[j], total)
    products_ref[...] = total.astype(BF16).reshape(products_ref.shape)
    arrive(2, half - 1)
    for t in range(3):
        for k in range(half):
            for copy in flying[t, k]:
                copy.wait_send()


ANY = pl.BlockSpec(memory_space=pl.ANY)
VMEM_LIMIT = 60 * 2**20


def gather_call(sections, owners, act, stash, cot, gain, dense, wg, wu, wd):
    tokens, width = stash.shape
    local, _, units = wg.shape
    half = owners // 2
    every = jax.ShapeDtypeStruct((owners, tokens, width), BF16)
    inner = jax.ShapeDtypeStruct((local, owners * tokens, units), BF16)
    small = jax.ShapeDtypeStruct((owners,) + dense.shape, BF16)
    return pl.pallas_call(
        functools.partial(gather_kernel, sections, owners),
        out_shape=(
            jax.ShapeDtypeStruct((tokens, width), BF16),
            every, every, every, small, inner, inner, inner, every, small,
        ),
        in_specs=[VMEM] * 5 + [ANY] * 3,
        out_specs=(VMEM,) * 10,
        scratch_shapes=[
            pltpu.VMEM(wg.shape, BF16),
            pltpu.VMEM(wu.shape, BF16),
            pltpu.VMEM(wd.shape, BF16),
            pltpu.VMEM(inner.shape, F32),
            pltpu.VMEM(inner.shape, F32),
            pltpu.VMEM((local, owners * tokens, LANES), F32),
            pltpu.SemaphoreType.DMA((2,)),
            pltpu.SemaphoreType.DMA((2,)),
            pltpu.SemaphoreType.DMA((owners - 1,)),
            pltpu.SemaphoreType.DMA((owners - 1,)),
            pltpu.SemaphoreType.DMA((3, 2, half)),
            pltpu.SemaphoreType.DMA((3, 2, half)),
            pltpu.SemaphoreType.DMA((3,)),
        ],
        compiler_params=pltpu.CompilerParams(
            collective_id=0, has_side_effects=True, vmem_limit_bytes=VMEM_LIMIT
        ),
    )(act, stash, cot, gain, dense, wg, wu, wd)


def reduce_kernel(
    sections, owners,
    row_ref, products_ref, next_ref, prev_ref, cots_ref, gates_ref,
    d_gate_ref, d_up_ref, gated_ref, wg_hbm, wu_hbm, wd_hbm,
    summed_ref, mixed_ref, returned_ref, grad_gate_hbm, grad_up_hbm, grad_down_hbm,
    wg, wu, wd, hidden_ref, part_ref,
    outgoing, arriving, small_send, small_recv, ring_send, ring_recv, weight_sem, grad_sem,
):
    parts, totals, count = (row_ref, part_ref), (summed_ref, mixed_ref), 2
    local, _, units = wg.shape
    loads = load_weights((wg_hbm, wu_hbm, wd_hbm), (wg, wu, wd), weight_sem)
    ring = Ring(sections, owners)
    me, half = ring.me, ring.half
    width = parts[0].shape[2]
    cut = width // 2
    ring.greet(False)

    def start(t, k):
        made = []
        for d, way in enumerate((1, -1)):
            block = ring.owner(way * (half - k))
            cols = pl.ds(d * cut, cut)
            if k == 0:
                src = parts[t].at[block, :, cols]
                dst = arriving.at[t, d, k, :, cols]
            else:
                src, dst = outgoing.at[t, d, k - 1], arriving.at[t, d, k]
                if k == 1:
                    rest = pl.ds((1 - d) * cut, cut)
                    src[:, rest] = parts[t][block, :, rest]
                    src[:, cols] = (
                        parts[t][block, :, cols].astype(F32)
                        + arriving[t, d, k - 1, :, cols].astype(F32)
                    ).astype(BF16)
                else:
                    src[...] = (
                        parts[t][block].astype(F32) + arriving[t, d, k - 1].astype(F32)
                    ).astype(BF16)
            made.append(
                send(src, dst, ring_send.at[t, d, k], ring_recv.at[t, d, k], ring.device(ring.sides[d]))
            )
            made[-1].start()
        flying[t, k] = made

    flying = {}
    start(0, 0)
    small = [
        send(
            products_ref.at[ring.peer(r)], returned_ref.at[me],
            small_send.at[r - 1], small_recv.at[r - 1], ring.device(ring.peer(r)),
        )
        for r in range(1, owners)
    ]
    for copy in small:
        copy.start()
    returned_ref[me] = products_ref[me]
    def advance(t, k):
        if k < half:
            for copy in flying[t, k - 1]:
                copy.wait_recv()
            start(t, k)

    def finish(t):
        for copy in flying[t, half - 1]:
            copy.wait_recv()
        totals[t][...] = (
            parts[t][me].astype(F32)
            + arriving[t, 0, half - 1].astype(F32)
            + arriving[t, 1, half - 1].astype(F32)
        )

    tile, wide = tile_of(units), tile_of(width)

    def hidden(j):
        weight = gate_column(gates_ref, me * local + j)

        @pl.loop(0, units // tile)
        def _(i):
            cols = columns(i, tile)
            rows = flat(next_ref)
            gate = dot(rows, wg[j, :, cols], 1, 0)
            up = dot(rows, wu[j, :, cols], 1, 0)
            hidden_ref[j, :, cols] = (weight * (gate * jax.nn.sigmoid(gate) * up)).astype(BF16)

    def mix(low, high):
        @pl.loop(low, high)
        def _(i):
            cols = columns(i, wide)
            total = 0.0
            for j in range(local):
                total = total + dot(hidden_ref[j], wd[j, :, cols], 1, 0)
            part_ref[:, :, cols] = total.astype(BF16).reshape(part_ref.shape[:2] + (wide,))

    grads = []

    def weight_gradient(held, out_hbm, index, j):
        rows_size = held.shape[1]
        step = tile_of(rows_size)

        @pl.loop(0, rows_size // step)
        def _(i):
            rows = columns(i, step)
            if index == 2:
                left, right = gated_ref[j, :, rows], flat(cots_ref)
            else:
                left = prev_ref[:, :, rows].reshape(-1, step)
                right = (d_gate_ref, d_up_ref)[index][j]
            held[j, rows, :] = dot(left, right, 0, 0).astype(BF16)

        copy = pltpu.make_async_copy(held.at[j], out_hbm.at[j], grad_sem.at[index, j])
        copy.start()
        grads.append(copy)

    for copy in loads:
        copy.wait()
    for j in range(local):
        hidden(j)
    advance(0, 1)
    mix(0, width // wide)
    start(1, 0)
    advance(0, 2)
    hops = []
    for k in range(1, half):
        hops += [(1, k), (0, k + 2)]
    hops = [(t, k) for t, k in hops if k < half]
    for index, (held, out) in enumerate(((wg, grad_gate_hbm), (wu, grad_up_hbm), (wd, grad_down_hbm))):
        for j in range(local):
            weight_gradient(held, out, index, j)
            if hops:
                advance(*hops.pop(0))
    for hop in hops:
        advance(*hop)
    finish(0)
    finish(1)
    for copy in grads:
        copy.wait()
    for t in range(count):
        for k in range(half):
            for copy in flying[t, k]:
                copy.wait_send()
    for copy in small:
        copy.wait()


def reduce_call(sections, owners, row, products, rows_next, prev, cots, gates, inner, weights):
    _, tokens, width = row.shape
    half = owners // 2
    total = jax.ShapeDtypeStruct((tokens, width), F32)
    return pl.pallas_call(
        functools.partial(reduce_kernel, sections, owners),
        out_shape=(total, total, jax.ShapeDtypeStruct(products.shape, BF16))
        + tuple(jax.ShapeDtypeStruct(w.shape, BF16) for w in weights),
        in_specs=[VMEM] * 9 + [ANY] * 3,
        out_specs=(VMEM,) * 3 + (ANY,) * 3,
        scratch_shapes=[pltpu.VMEM(w.shape, BF16) for w in weights]
        + [
            pltpu.VMEM(inner[0].shape, BF16),
            pltpu.VMEM(row.shape, BF16),
            pltpu.VMEM((2, 2, half - 1, tokens, width), BF16),
            pltpu.VMEM((2, 2, half, tokens, width), BF16),
            pltpu.SemaphoreType.DMA((owners - 1,)),
            pltpu.SemaphoreType.DMA((owners - 1,)),
            pltpu.SemaphoreType.DMA((2, 2, half)),
            pltpu.SemaphoreType.DMA((2, 2, half)),
            pltpu.SemaphoreType.DMA((3,)),
            pltpu.SemaphoreType.DMA((3, weights[0].shape[0])),
        ],
        compiler_params=pltpu.CompilerParams(
            collective_id=1, has_side_effects=True, vmem_limit_bytes=VMEM_LIMIT
        ),
    )(row, products, rows_next, prev, cots, gates, *inner, *weights)


def apply_rms_norm(rows, gain):
    values = rows.astype(F32)
    scale = lax.rsqrt(jnp.mean(values * values, axis=-1, keepdims=True) + EPS)
    unit = values * scale
    return (unit * gain).astype(BF16), unit, scale


def dense_gates(routes, gates, experts_all):
    hit = routes[:, :, None] == jnp.arange(experts_all, dtype=jnp.int32)
    return jnp.sum(jnp.where(hit, gates.astype(F32)[:, :, None], 0.0), axis=1).astype(BF16)


def per_device(
    sent_acts,
    stash,
    cotangents,
    norm_gain,
    w_gate,
    w_up,
    w_down,
    routes_next,
    gates_next,
    routes_prev,
    gates_prev,
):
    owners = lax.axis_size("expert")
    me = lax.axis_index("expert")
    gain = norm_gain[0].astype(F32)
    wg, wu, wd = w_gate[0], w_up[0], w_down[0]
    local, width, hidden_units = wg.shape
    experts_all = local * owners
    tokens = stash.shape[1]

    dense = jnp.concatenate(
        [
            dense_gates(routes_next[0], gates_next[0], experts_all),
            dense_gates(routes_prev[0], gates_prev[0], experts_all),
        ],
        axis=1,
    )
    dense = jnp.pad(dense, ((0, 0), (0, LANES - dense.shape[1])))
    sections = lax.axis_size("section")
    _, unit_rows, scale = apply_rms_norm(stash[0], gain)
    weights = (wg, wu, wd)
    arrived, next_all, prev_all, cot_all, dense_all, d_gate, d_up, gated, row, products = gather_call(
        sections, owners, sent_acts[0], stash[0], cotangents[0], gain[None], dense, *weights
    )
    cot = lax.dynamic_index_in_dim(cot_all, me, 0, keepdims=False)
    summed, mixed, products_back, grad_gate, grad_up, grad_down = reduce_call(
        sections, owners, row, products, next_all, prev_all, cot_all, dense_all,
        (d_gate, d_up, gated), weights,
    )
    products_back = products_back[:, :, :local]

    fwd_out = (arrived.astype(F32) + mixed).astype(BF16)

    by_expert = jnp.transpose(products_back, (1, 0, 2)).reshape(tokens, experts_all).astype(F32)
    hit = routes_prev[0][:, :, None] == jnp.arange(experts_all, dtype=jnp.int32)
    gate_grad = jnp.sum(jnp.where(hit, by_expert[:, None, :], 0.0), axis=-1).astype(BF16)

    normalized_gradient = summed * gain
    backward = cot.astype(F32) + scale * (
        normalized_gradient
        - unit_rows * jnp.mean(normalized_gradient * unit_rows, axis=-1, keepdims=True)
    )
    return (
        fwd_out[None],
        backward.astype(BF16)[None],
        gate_grad[None],
        grad_gate[None],
        grad_up[None],
        grad_down[None],
    )


def solution(mesh):
    tokens = P("section", "expert", None)
    weights = P("section", "expert", None, None)
    return jax.shard_map(
        per_device,
        mesh=mesh,
        in_specs=(tokens, tokens, tokens, P("section", None), weights, weights, weights)
        + (tokens,) * 4,
        out_specs=(tokens, tokens, tokens, weights, weights, weights),
        check_vma=False,
    )
```

profile of v0, /device:TPU:0, one launch (start us, length us, event | category | flops | bytes accessed | tf_op | source)
XLA Modules:
  0.0 167.4 jit_solution(2777363204694695845)
XLA Ops:
  0.6 0.7 bitcast_convert_fusion
  1.3 0.7 select_reduce_fusion.1
  2.0 0.1 copy.31
  2.1 0.7 bitcast_convert_fusion.1
  2.8 0.7 select_reduce_fusion.2
  3.5 0.1 copy.30
  3.6 0.7 fusion.12.dense_ref
  4.3 1.3 convert_element_type.76.gain_ref
  5.6 84.1 %shard_map.154 = (bf16[64,2048]{1,0:T(8,128)(2,1)}, bf16[8,64,2048]{2,1,0:T(8,128)(2,1)}, bf16[8,64,2048]{2,1,0:T(8,128)(2,1)}, bf16[8,64,2048]{2,1,0:T(8,128)(2...) custom-call(bf16[64,2048]{1,0:T(8,128)(2,1)} %bitcast.48, ...), custom_call_target="tpu_custom_call" | custom-call | tf_op jit(solution)/shard_map/pallas_call | solution.py:249
  89.7 0.0 copy-start
  89.7 0.0 copy-start.2
  89.7 0.0 copy-start.3
  89.7 59.5 %shard_map.155 = (f32[64,2048]{1,0:T(8,128)}, f32[64,2048]{1,0:T(8,128)}, bf16[8,64,128]{2,1,0:T(8,128)(2,1)}, bf16[2,2048,768]{2,1,0:T(8,128)(2,1)}, bf16[2,204...) custom-call(bf16[8,64,2048]{2,1,0:T(8,128)(2,1)} %get-tuple-element.23.row_ref, ...), custom_call_target="tpu_custom_call" | custom-call | tf_op jit(solution)/shard_map/pallas_call | solution.py:426
  149.3 0.2 fusion.7
  149.5 1.3 fusion.2
  150.8 0.0 slice-start.2
  150.8 2.4 %fusion.8 = (bf16[1,64,2048]{2,1,0:T(8,128)(2,1)}, bf16[1,64,2048]{2,1,0:T(8,128)(2,1)}) fusion(f32[64,2048]{1,0:T(8,128)} %get-tuple-element.32, bf16[64,2048]{1,0:T(8,128)(2,1)S(1)} %copy-done.1, f32[64]{0:T(128)S(1)} %broadcast_multiply_fusion, bf16[1,64,2048]{2,1,0:T(8,128)(2,1)S(1)} %copy-done, f32[64,2048]{1,0:T(8,128)} %get-tuple-element.33, ...), kind=kLoop, calls=%fused_computation.11 | loop fusion | flops 1572864 | bytes 2368004 | tf_op jit(solution)/shard_map/broadcast_in_dim | solution.py:517
  153.2 0.9 convert_bitcast_fusion
  154.1 0.1 copy.32
  154.3 0.6 select_reduce_fusion
  154.9 6.5 %copy.36 = bf16[1,2,2048,768]{3,2,1,0:T(8,128)(2,1)} copy(bf16[1,2,2048,768]{3,2,1,0:T(8,128)(2,1)} %bitcast.46) | data formatting | bytes 12582912
  161.4 2.8 %copy.37 = bf16[1,2,2048,768]{3,2,1,0:T(8,128)(2,1)} copy(bf16[1,2,2048,768]{3,2,1,0:T(8,128)(2,1)S(1)} %bitcast.45) | data formatting | bytes 12582912
  164.2 0.5 slice-done.1
  164.7 2.7 %copy.38 = bf16[1,2,768,2048]{3,2,1,0:T(8,128)(2,1)} copy(bf16[1,2,768,2048]{3,2,1,0:T(8,128)(2,1)S(1)} %bitcast.42) | data formatting | bytes 12582912
  (15 shorter events, 0.0 us)
Async XLA Ops:
  89.7 59.6 %copy-start = (bf16[1,64,2048]{2,1,0:T(8,128)(2,1)S(1)}, bf16[1,64,2048]{2,1,0:T(8,128)(2,1)}, u32[]{:S(2)}) copy-start(bf16[1,64,2048]{2,1,0:T(8,128)(2,1)} %param.12) | copy-start | bytes 786436
  89.7 59.8 %copy-start.2 = (f32[1,2048]{1,0:T(1,128)S(1)}, f32[1,2048]{1,0:T(1,128)}, u32[]{:S(2)}) copy-start(f32[1,2048]{1,0:T(1,128)} %convert_element_type.76.gain_ref) | copy-start | bytes 24580
  89.7 61.1 %copy-start.1 = (bf16[64,2048]{1,0:T(8,128)(2,1)S(1)}, bf16[64,2048]{1,0:T(8,128)(2,1)}, u32[]{:S(2)}) copy-start(bf16[64,2048]{1,0:T(8,128)(2,1)} %get-tuple-element.22) | copy-start | bytes 786436
  89.7 64.5 %copy-start.3 = (s32[1,64,8]{1,2,0:T(8,128)S(1)}, s32[1,64,8]{1,2,0:T(8,128)}, u32[]{:S(2)}) copy-start(s32[1,64,8]{1,2,0:T(8,128)} %param.20) | copy-start | bytes 6148
  150.8 10.7 %slice-start.2 = ((s8[6291456]{0:T(1024)(128)(4,1)}), s8[2097152]{0:T(1024)(128)(4,1)S(1)}, s32[]{:S(2)}) async-start(s8[6291456]{0:T(1024)(128)(4,1)} %bitcast.43), calls=%async_computation.2 | async-start | bytes 4194304
  154.9 6.5 %slice-start.3 = ((s8[6291456]{0:T(1024)(128)(4,1)}), s8[4194304]{0:T(1024)(128)(4,1)S(1)}, s32[]{:S(2)}) async-start(s8[6291456]{0:T(1024)(128)(4,1)} %bitcast.43), calls=%async_computation.3 | async-start | bytes 8388608
  154.9 9.4 %slice-start = ((s8[6291456]{0:T(1024)(128)(4,1)}), s8[4194304]{0:T(1024)(128)(4,1)S(1)}, s32[]{:S(2)}) async-start(s8[6291456]{0:T(1024)(128)(4,1)} %bitcast.40), calls=%async_computation | async-start | bytes 8388608
  161.4 3.3 %slice-start.1 = ((s8[6291456]{0:T(1024)(128)(4,1)}), s8[2097152]{0:T(1024)(128)(4,1)S(1)}, s32[]{:S(2)}) async-start(s8[6291456]{0:T(1024)(128)(4,1)} %bitcast.40), calls=%async_computation.1 | async-start | bytes 4194304
where the time goes:
time: 168 us; the launch traced here: 167 us
  Pallas kernels  144 us (86%)
  local copies, waits for them, and re-layouts  12.9 us (8%)
  other arithmetic  10.2 us (6%)
    pallas_call x1, Pallas kernels, gather_call(): pl.pallas_call(functools.partial(gather_kernel, sections, owners), out_sh...  84.1 us
    pallas_call x1, Pallas kernels, reduce_call(): pl.pallas_call(functools.partial(reduce_kernel, sections, owners), out_sh...  59.5 us
    unnamed x19, local copies, waits for them, and re-layouts  12.5 us

commit v1 on v0

v1 whole, which is shorter than its diff:
```python
import functools

import jax
import jax.numpy as jnp
from jax import lax
from jax.experimental import pallas as pl
from jax.experimental.pallas import tpu as pltpu
from jax.sharding import PartitionSpec as P

EPS = 1e-06
F32 = jnp.float32
BF16 = jnp.bfloat16
LANES = 128
GROUP = 16
CHUNKS = 2
PREV, COT, NEXT = 0, 1, 2
ROW, MIX = 0, 1
VMEM = pl.BlockSpec(memory_space=pltpu.VMEM)
ANY = pl.BlockSpec(memory_space=pl.ANY)
VMEM_LIMIT = 61 * 2**20


class Ring:
    def __init__(self, sections, owners):
        bits = owners.bit_length() - 1
        self.n = owners
        self.half = owners // 2
        self.nz = 1 << ((bits + 1) // 2)
        self.ny = owners // self.nz
        self.section = lax.axis_index("section")
        self.sections = sections
        self.me = lax.axis_index("expert")
        z, y = self.me // self.ny, self.me % self.ny
        self.place = y * self.nz + z + (y % 2) * (self.nz - 1 - 2 * z)
        self.sides = (self.device(1), self.device(-1))

    def device(self, offset):
        p = (self.place + offset + self.n) % self.n
        y, r = p // self.nz, p % self.nz
        return (self.section, (r + (y % 2) * (self.nz - 1 - 2 * r)) * self.ny + y)

    def shifted(self, by):
        return ((self.section + by + self.sections) % self.sections, self.me)

    def slot(self, offset):
        offset = (offset + self.n) % self.n
        if offset > self.half:
            return 2 * (self.n - offset) - 1
        return 2 * offset - (offset == self.half)

    def greet(self):
        barrier = pltpu.get_barrier_semaphore()
        targets = [self.device(r) for r in range(1, self.n)]
        targets += [self.shifted(1), self.shifted(-1)]
        for target in targets:
            pl.semaphore_signal(
                barrier, inc=1, device_id=target, device_id_type=pl.DeviceIdType.MESH
            )
        return lambda: pl.semaphore_wait(barrier, len(targets))


def send(src, dst, send_sem, recv_sem, device):
    return pltpu.make_async_remote_copy(
        src_ref=src,
        dst_ref=dst,
        send_sem=send_sem,
        recv_sem=recv_sem,
        device_id=device,
        device_id_type=pl.DeviceIdType.MESH,
    )


def scale_of(values):
    return lax.rsqrt(jnp.mean(values * values, axis=-1, keepdims=True) + EPS)


def dot(a, b, ca, cb):
    return lax.dot_general(a, b, (((ca,), (cb,)), ((), ())), preferred_element_type=F32)


def flat(ref):
    value = ref[...]
    return value.reshape(-1, value.shape[-1])


def tile_of(size):
    return 256 if size % 256 == 0 else LANES


def span(i, size):
    return pl.ds(pl.multiple_of(i * size, size), size)


def eye(size):
    shape = (size, size)
    row, col = (lax.broadcasted_iota(jnp.int32, shape, d) for d in range(2))
    return (row == col).astype(BF16)


def run(count, body, actions=()):
    table = {}
    for n, action in enumerate(actions):
        table.setdefault((2 * n + 1) * count // (2 * len(actions)), []).append(action)

    @pl.loop(0, count)
    def _(i):
        for at, group in table.items():
            @pl.when(i == at)
            def _():
                for action in group:
                    action()
        body(i)


def tick_kernel(
    sections, owners,
    act_ref, stash_ref, cot_ref, gain_ref,
    routes_next_ref, choice_next_ref, routes_prev_ref, choice_prev_ref,
    wg_hbm, wu_hbm, wd_hbm,
    fwd_ref, bwd_ref, gate_grad_ref, wg, wu, wd,
    arrived_ref, prev_ref, cots_ref, next_ref, row_ref, part_ref, arriving,
    gates_ref, products_ref, returned_ref, weight_ref, sums,
    pre_gate, pre_up, d_gate, d_up, gated, hidden_ref,
    shift_send, shift_recv, gate_send, gate_recv, product_send, product_recv,
    gather_send, gather_recv, reduce_send, reduce_recv, weight_sem,
):
    ring = Ring(sections, owners)
    half = ring.half
    tokens, width = stash_ref.shape
    local, _, units = wg.shape
    experts = local * owners
    chunk = width // CHUNKS
    loads = [
        pltpu.make_async_copy(h, v, weight_sem.at[i])
        for i, (h, v) in enumerate(((wg_hbm, wg), (wu_hbm, wu), (wd_hbm, wd)))
    ]
    for copy in loads:
        copy.start()
    met = ring.greet()

    def normalize(source, target):
        @pl.loop(0, tokens // GROUP)
        def _(i):
            rows = span(i, GROUP)
            values = source[rows, :].astype(F32)
            target[0, rows, :] = (values * scale_of(values) * gain_ref[...].astype(F32)).astype(BF16)

    def dense_gates():
        lane = lax.broadcasted_iota(jnp.int32, (LANES, tokens), 0)
        total = jnp.zeros((LANES, tokens), F32)
        for base, routes, gates in (
            (0, routes_next_ref, choice_next_ref), (experts, routes_prev_ref, choice_prev_ref)
        ):
            names, values = routes[...] + base, gates[...].astype(F32)
            for k in range(names.shape[0]):
                total += jnp.where(names[k : k + 1] == lane, values[k : k + 1], 0.0)
        gates_ref[0] = dot(eye(tokens), total.astype(BF16), 1, 1).astype(BF16)

    buffers, parts = (prev_ref, cots_ref, next_ref), (row_ref, part_ref)
    ways = ((0, 1), (1, -1))

    def columns(c, d, cut):
        return pl.ds(c * chunk + d * (chunk // 2), chunk // 2) if cut else pl.ds(c * chunk, chunk)

    def gather(t, c, k):
        copies = []
        for d, way in ways:
            cols = columns(c, d, k == half - 1)
            copies.append(send(
                buffers[t].at[ring.slot(-way * k), :, cols],
                buffers[t].at[ring.slot(-way * (k + 1)), :, cols],
                gather_send.at[t, c, d, k], gather_recv.at[t, c, d, k], ring.sides[d],
            ))
        return copies

    def reduce(t, c, k):
        copies = []
        for d, way in ways:
            cols = columns(c, d, k == 0)
            copies.append(send(
                parts[t].at[ring.slot(way * (half - k)), :, cols],
                arriving.at[t, d, k, :, cols],
                reduce_send.at[t, c, d, k], reduce_recv.at[t, c, d, k], ring.sides[d],
            ))
        return copies

    def go(copies):
        for copy in copies:
            copy.start()

    def come(copies):
        for copy in copies:
            copy.wait_recv()

    def pass_on(t, c, k):
        def action():
            if k > 0:
                come(gather(t, c, k - 1))
            go(gather(t, c, k))
        return action

    def add_on(t, c, k):
        def action():
            if k > 0:
                come(reduce(t, c, k - 1))
                for d, way in ways:
                    slot, cols = ring.slot(way * (half - k)), columns(c, d, k == 1)
                    parts[t][slot, :, cols] = (
                        parts[t][slot, :, cols].astype(F32)
                        + arriving[t, d, k - 1, :, cols].astype(F32)
                    ).astype(BF16)
            go(reduce(t, c, k))
        return action

    def total_of(t, rows):
        return (
            parts[t][0, rows, :].astype(F32)
            + arriving[t, 0, half - 1, rows, :].astype(F32)
            + arriving[t, 1, half - 1, rows, :].astype(F32)
        )

    def weights_of(base):
        rows = flat(gates_ref).astype(F32)
        lane = lax.broadcasted_iota(jnp.int32, rows.shape, 1)
        for j in range(local):
            index = base + ring.me * local + j
            column = jnp.sum(jnp.where(lane == index, rows, 0.0), axis=1, keepdims=True)
            weight_ref[base // experts, j] = jnp.broadcast_to(column, rows.shape)

    tile, wide = tile_of(units), tile_of(width)
    inner = units // tile

    def weight_of(m, j):
        return jnp.concatenate([weight_ref[m, j]] * (tile // LANES), axis=1)

    def pre_activation(n):
        j, cols = n // inner, span(n % inner, tile)
        rows = flat(prev_ref)
        pre_gate[j, :, cols] = dot(rows, wg[j, :, cols], 1, 0)
        pre_up[j, :, cols] = dot(rows, wu[j, :, cols], 1, 0)

    def gradient(n):
        j, cols = n // inner, span(n % inner, tile)
        weight = weight_of(1, j)
        plain = dot(flat(cots_ref), wd[j, cols, :], 1, 1)
        gate, up = pre_gate[j, :, cols], pre_up[j, :, cols]
        sigma = jax.nn.sigmoid(gate)
        active = gate * sigma
        hidden = active * up
        d_hidden = weight * plain
        product = hidden * plain
        for i in range(tile // LANES):
            sums[j] += product[:, i * LANES : (i + 1) * LANES]
        gated[j, :, cols] = (weight * hidden).astype(BF16)
        d_gate[j, :, cols] = (d_hidden * up * sigma * (1.0 + gate * (1.0 - sigma))).astype(BF16)
        d_up[j, :, cols] = (d_hidden * active).astype(BF16)

    def row_gradient(first):
        def body(n):
            cols = span(first + n, wide)
            total = 0.0
            for j in range(local):
                total = total + dot(d_gate[j], wg[j, cols, :], 1, 1)
                total = total + dot(d_up[j], wu[j, cols, :], 1, 1)
            row_ref[:, :, cols] = total.astype(BF16).reshape(owners, tokens, wide)
        return body

    def hidden(n):
        j, cols = n // inner, span(n % inner, tile)
        rows = flat(next_ref)
        gate = dot(rows, wg[j, :, cols], 1, 0)
        up = dot(rows, wu[j, :, cols], 1, 0)
        hidden_ref[j, :, cols] = (
            weight_of(0, j) * (gate * jax.nn.sigmoid(gate) * up)
        ).astype(BF16)

    def mix(first):
        def body(n):
            cols = span(first + n, wide)
            total = 0.0
            for j in range(local):
                total = total + dot(hidden_ref[j], wd[j, :, cols], 1, 0)
            part_ref[:, :, cols] = total.astype(BF16).reshape(owners, tokens, wide)
        return body

    steps, deep = width // wide, units // tile

    def outer_gradient(n):
        j, rows = n // steps, span(n % steps, wide)
        left = prev_ref[:, :, rows].reshape(-1, wide)
        wg[j, rows, :] = dot(left, d_gate[j], 0, 0).astype(BF16)
        wu[j, rows, :] = dot(left, d_up[j], 0, 0).astype(BF16)

    def down_gradient(n):
        j, rows = n // deep, span(n % deep, tile)
        wd[j, rows, :] = dot(gated[j, :, rows], flat(cots_ref), 0, 0).astype(BF16)

    def small(source, target, sends, receives, own):
        return [
            send(
                source.at[0 if own else ring.slot(r)], target.at[ring.slot(-r)],
                sends.at[r - 1], receives.at[r - 1], ring.device(r),
            )
            for r in range(1, owners)
        ]

    def return_products():
        lane = lax.broadcasted_iota(jnp.int32, sums.shape[1:], 1)
        total = jnp.zeros(sums.shape[1:], F32)
        for j in range(local):
            column = jnp.sum(sums[j], axis=1, keepdims=True)
            total = jnp.where(lane == ring.me * local + j, column, total)
        products_ref[...] = total.astype(BF16).reshape(products_ref.shape)
        go(small(products_ref, returned_ref, product_send, product_recv, False))
        returned_ref[0] = products_ref[0]

    def backward():
        come(small(products_ref, returned_ref, product_send, product_recv, False))
        by_expert = jnp.sum(returned_ref[...].astype(F32), axis=0).astype(BF16)
        turned = dot(eye(LANES), by_expert, 1, 1)
        name = lax.broadcasted_iota(jnp.int32, turned.shape, 0)
        names = routes_prev_ref[...]
        picks = [
            jnp.sum(jnp.where(names[k : k + 1] == name, turned, 0.0), axis=0, keepdims=True)
            for k in range(names.shape[0])
        ]
        gate_grad_ref[...] = jnp.concatenate(picks, axis=0).astype(BF16)
        for c in range(CHUNKS):
            come(reduce(ROW, c, half - 1))

        @pl.loop(0, tokens // GROUP)
        def _(i):
            rows = span(i, GROUP)
            values = stash_ref[rows, :].astype(F32)
            scale = scale_of(values)
            unit = values * scale
            change = total_of(ROW, rows) * gain_ref[...].astype(F32)
            mean = jnp.mean(change * unit, axis=-1, keepdims=True)
            bwd_ref[rows, :] = (
                cots_ref[0, rows, :].astype(F32) + scale * (change - unit * mean)
            ).astype(BF16)

    def forward():
        for c in range(CHUNKS):
            come(reduce(MIX, c, half - 1))

        @pl.loop(0, tokens // GROUP)
        def _(i):
            rows = span(i, GROUP)
            fwd_ref[rows, :] = (arrived_ref[rows, :].astype(F32) + total_of(MIX, rows)).astype(BF16)

    cot_shift = send(cot_ref, cots_ref.at[0], shift_send.at[0], shift_recv.at[0], ring.shifted(-1))
    act_shift = send(act_ref, arrived_ref, shift_send.at[1], shift_recv.at[1], ring.shifted(1))
    both = range(CHUNKS)

    normalize(stash_ref, prev_ref)
    dense_gates()
    met()
    cot_shift.start()
    for c in both:
        pass_on(PREV, c, 0)()
    gate_copies = small(gates_ref, gates_ref, gate_send, gate_recv, True)
    go(gate_copies)
    sums[...] = jnp.zeros(sums.shape, F32)
    cot_shift.wait()
    act_shift.start()
    for c in both:
        pass_on(COT, c, 0)()
    for k in range(1, half):
        for c in both:
            pass_on(PREV, c, k)()
        if k == 1:
            act_shift.wait()
            normalize(arrived_ref, next_ref)
    cots = [pass_on(COT, c, k) for k in range(1, half) for c in both]
    nexts = [pass_on(NEXT, c, k) for k in range(half) for c in both]
    for action in cots[:CHUNKS] + nexts[:1]:
        action()
    come(gate_copies)
    for base in (0, experts):
        weights_of(base)
    for copy in loads:
        copy.wait()
    for c in both:
        come(gather(PREV, c, half - 1))
    run(local * inner, pre_activation, cots[CHUNKS:-CHUNKS])
    for action in (cots[-2], nexts[1], cots[-1], nexts[2]):
        action()
    for c in both:
        come(gather(COT, c, half - 1))
    split = steps // CHUNKS
    run(local * inner, gradient, nexts[3:-2])
    run(split, row_gradient(0), nexts[-2:-1])
    add_on(ROW, 0, 0)()
    nexts[-1]()
    for c in range(1, CHUNKS):
        run(split, row_gradient(c * split))
        add_on(ROW, c, 0)()
    return_products()
    for c in both:
        come(gather(NEXT, c, half - 1))
    rows = [add_on(ROW, c, k) for k in range(1, half) for c in both]
    mixes = [add_on(MIX, c, k) for k in range(1, half) for c in both]
    run(local * inner, hidden, rows[:-CHUNKS])
    for c in both:
        run(split, mix(c * split), rows[c - CHUNKS : len(rows) + c - CHUNKS + 1])
        add_on(MIX, c, 0)()
    backward()
    run(local * steps, outer_gradient, mixes[:-CHUNKS])
    run(local * deep, down_gradient, mixes[-CHUNKS:])
    forward()
    for c in both:
        for k in range(half):
            for copies in [gather(t, c, k) for t in range(3)] + [reduce(t, c, k) for t in range(2)]:
                for copy in copies:
                    copy.wait_send()
    act_products = small(products_ref, returned_ref, product_send, product_recv, False)
    for copy in gate_copies + act_products:
        copy.wait_send()


def tick_call(sections, owners, act, stash, cot, gain, choices, weights):
    tokens, width = stash.shape
    local, _, units = weights[0].shape
    half = owners // 2
    every = pltpu.VMEM((owners, tokens, width), BF16)
    inner = (local, owners * tokens, units)
    lanes = (local, owners * tokens, LANES)
    small = pltpu.VMEM((owners, tokens, LANES), BF16)
    peers = pltpu.SemaphoreType.DMA((owners - 1,))
    held = sum(w.size for w in weights) * jnp.dtype(BF16).itemsize
    return pl.pallas_call(
        functools.partial(tick_kernel, sections, owners),
        out_shape=(
            pltpu.VMEM((tokens, width), BF16),
            pltpu.VMEM((tokens, width), BF16),
            pltpu.VMEM(choices[0].shape, BF16),
        )
        + tuple(pltpu.VMEM(w.shape, BF16) for w in weights),
        in_specs=[VMEM] * 8 + [ANY] * 3,
        out_specs=(VMEM,) * 6,
        scratch_shapes=[pltpu.VMEM((tokens, width), BF16)]
        + [every] * 5
        + [pltpu.VMEM((2, 2, half, tokens, width), BF16)]
        + [small] * 3
        + [pltpu.VMEM((2,) + lanes, F32), pltpu.VMEM(lanes, F32)]
        + [pltpu.VMEM(inner, F32)] * 2
        + [pltpu.VMEM(inner, BF16)] * 4
        + [pltpu.SemaphoreType.DMA((2,))] * 2
        + [peers] * 4
        + [pltpu.SemaphoreType.DMA((3, CHUNKS, 2, half))] * 2
        + [pltpu.SemaphoreType.DMA((2, CHUNKS, 2, half))] * 2
        + [pltpu.SemaphoreType.DMA((3,))],
        compiler_params=pltpu.CompilerParams(
            collective_id=0, has_side_effects=True, vmem_limit_bytes=VMEM_LIMIT - held
        ),
    )(act, stash, cot, gain, *choices, *weights)


def per_device(
    sent_acts,
    stash,
    cotangents,
    norm_gain,
    w_gate,
    w_up,
    w_down,
    routes_next,
    gates_next,
    routes_prev,
    gates_prev,
):
    choices = [jnp.swapaxes(a[0], 0, 1) for a in (routes_next, gates_next, routes_prev, gates_prev)]
    fwd, bwd, gate_grad, *grads = tick_call(
        lax.axis_size("section"), lax.axis_size("expert"),
        sent_acts[0], stash[0], cotangents[0], norm_gain, choices, (w_gate[0], w_up[0], w_down[0]),
    )
    return (fwd[None], bwd[None], jnp.swapaxes(gate_grad, 0, 1)[None]) + tuple(g[None] for g in grads)


def solution(mesh):
    tokens = P("section", "expert", None)
    weights = P("section", "expert", None, None)
    return jax.shard_map(
        per_device,
        mesh=mesh,
        in_specs=(tokens, tokens, tokens, P("section", None), weights, weights, weights)
        + (tokens,) * 4,
        out_specs=(tokens, tokens, tokens, weights, weights, weights),
        check_vma=False,
    )
```

time: 168 us -> 128 us (0.76)
  Pallas kernels: 144 us -> 117 us
  other arithmetic: 10.2 us -> 0 us
  local copies, waits for them, and re-layouts: 12.9 us -> 10.1 us
    pallas_call x2 -> x1, Pallas kernels: 144 us -> 117 us  [tick_call(): pl.pallas_call(functools.partial(tick_kernel, sections, owners), out_shap...]
    convert_element_type x4 -> x0, other arithmetic: 3.6 us -> none  [the longest x2 1.37 us: dense_gates(): gates.astype(F32)[:, :, None]]
    reduce_sum x5 -> x0, other arithmetic: 3.46 us -> none  [the longest x2 1.4 us: dense_gates(): jnp.sum(jnp.where(hit, gates.astype(F32)[:, :, None], 0.0), axis=1)]
    unnamed x19 -> x6, local copies, waits for them, and re-layouts: 12.5 us -> 10.1 us
    broadcast_in_dim x1 -> x0, other arithmetic: 2.42 us -> none  [per_device(): fwd_out[None]]
where the time goes in v1:
time: 128 us
  Pallas kernels  117 us (91%)
  local copies, waits for them, and re-layouts  10.1 us (8%)
    pallas_call x1, Pallas kernels, tick_call(): pl.pallas_call(functools.partial(tick_kernel, sections, owners), out_shap...  117 us
    unnamed x6, local copies, waits for them, and re-layouts  10.1 us

profile of v1, /device:TPU:0, one launch (start us, length us, event | category | flops | bytes accessed | tf_op | source)
XLA Modules:
  0.0 127.7 jit_solution(18258997248358005726)
XLA Ops:
  0.6 117.0 %shard_map.154 = (bf16[64,2048]{1,0:T(8,128)(2,1)S(1)}, bf16[64,2048]{1,0:T(8,128)(2,1)S(1)}, bf16[8,64]{1,0:T(8,128)(2,1)S(1)}, bf16[2,2048,768]{2,1,0:T(8,128)...) custom-call(bf16[64,2048]{1,0:T(8,128)(2,1)} %bitcast.35, bf16[64,2048]{1,0:T(8,128)(2,1)} %bitcast.36, ...), custom_call_target="tpu_custom_call" | custom-call | tf_op jit(solution)/shard_map/pallas_call | solution.py:432
  117.6 0.7 copy.23
  118.3 0.7 copy.24
  119.0 0.6 copy.25
  119.6 2.7 %copy.26 = bf16[1,2,2048,768]{3,2,1,0:T(8,128)(2,1)} copy(bf16[1,2,2048,768]{3,2,1,0:T(8,128)(2,1)S(1)} %bitcast.28) | data formatting | bytes 12582912
  122.3 2.7 %copy.27 = bf16[1,2,2048,768]{3,2,1,0:T(8,128)(2,1)} copy(bf16[1,2,2048,768]{3,2,1,0:T(8,128)(2,1)S(1)} %bitcast.27) | data formatting | bytes 12582912
  125.0 2.7 %copy.28 = bf16[1,2,768,2048]{3,2,1,0:T(8,128)(2,1)} copy(bf16[1,2,768,2048]{3,2,1,0:T(8,128)(2,1)S(1)} %bitcast.26) | data formatting | bytes 12582912

commit v2 on v1

--- a/solution.py
+++ b/solution.py
@@ -18,6 +18,7 @@
 VMEM = pl.BlockSpec(memory_space=pltpu.VMEM)
 ANY = pl.BlockSpec(memory_space=pl.ANY)
 VMEM_LIMIT = 61 * 2**20
+STORE_LIMIT = 4 * 2**20
 
 
 class Ring:
@@ -457,6 +458,31 @@
     )(act, stash, cot, gain, *choices, *weights)
 
 
+def store_kernel(count, *refs):
+    sem = refs[2 * count]
+    copies = [
+        pltpu.make_async_copy(v.at[i], h.at[i], sem.at[n, i])
+        for n, (v, h) in enumerate(zip(refs[:count], refs[count : 2 * count]))
+        for i in range(v.shape[0])
+    ]
+    for copy in copies:
+        copy.start()
+    for copy in copies:
+        copy.wait()
+
+
+def store(arrays):
+    count, most = len(arrays), max(a.shape[0] for a in arrays)
+    return pl.pallas_call(
+        functools.partial(store_kernel, count),
+        out_shape=tuple(jax.ShapeDtypeStruct(a.shape, a.dtype) for a in arrays),
+        in_specs=[ANY] * count,
+        out_specs=(ANY,) * count,
+        scratch_shapes=[pltpu.SemaphoreType.DMA((count, most))],
+        compiler_params=pltpu.CompilerParams(vmem_limit_bytes=STORE_LIMIT),
+    )(*(pltpu.with_memory_space_constraint(a, pltpu.VMEM) for a in arrays))
+
+
 def per_device(
     sent_acts,
     stash,
@@ -475,7 +501,8 @@
         lax.axis_size("section"), lax.axis_size("expert"),
         sent_acts[0], stash[0], cotangents[0], norm_gain, choices, (w_gate[0], w_up[0], w_down[0]),
     )
-    return (fwd[None], bwd[None], jnp.swapaxes(gate_grad, 0, 1)[None]) + tuple(g[None] for g in grads)
+    fwd, bwd, gate_grad, *grads = store((fwd[None], bwd[None], gate_grad[None], *grads))
+    return (fwd, bwd, jnp.swapaxes(gate_grad, 1, 2)) + tuple(g[None] for g in grads)
 
 
 def solution(mesh):

time: 128 us -> 125 us (0.977)
  local copies, waits for them, and re-layouts: 10.1 us -> 0 us
  Pallas kernels: 117 us -> 124 us
    unnamed x6 -> x0, local copies, waits for them, and re-layouts: 10.1 us -> none
    pallas_call x0 -> x1, Pallas kernels: none -> 6.86 us  [store(): pl.pallas_call(functools.partial(store_kernel, count), out_shape=tuple((j...]
where the time goes in v2:
time: 125 us; the launch traced here: 124 us
  Pallas kernels  124 us (99%)
    pallas_call x1, Pallas kernels, tick_call(): pl.pallas_call(functools.partial(tick_kernel, sections, owners), out_shap...  117 us
    pallas_call x1, Pallas kernels, store(): pl.pallas_call(functools.partial(store_kernel, count), out_shape=tuple((j...  6.86 us

profile of v2, /device:TPU:0, one launch (start us, length us, event | category | flops | bytes accessed | tf_op | source)
XLA Modules:
  0.0 124.5 jit_solution(405728338989975330)
XLA Ops:
  0.6 117.0 %shard_map.154 = (bf16[64,2048]{1,0:T(8,128)(2,1)S(1)}, bf16[64,2048]{1,0:T(8,128)(2,1)S(1)}, bf16[8,64]{1,0:T(8,128)(2,1)S(1)}, bf16[2,2048,768]{2,1,0:T(8,128)...) custom-call(bf16[64,2048]{1,0:T(8,128)(2,1)} %bitcast.31, bf16[64,2048]{1,0:T(8,128)(2,1)} %bitcast.32, ...), custom_call_target="tpu_custom_call" | custom-call | tf_op jit(solution)/shard_map/pallas_call | solution.py:433
  117.6 6.9 %shard_map.155 = (bf16[1,64,2048]{2,1,0:T(8,128)(2,1)}, bf16[1,64,2048]{2,1,0:T(8,128)(2,1)}, bf16[1,8,64]{2,1,0:T(8,128)(2,1)}, bf16[2,2048,768]{2,1,0:T(8,128)...) custom-call(bf16[1,64,2048]{2,1,0:T(8,128)(2,1)S(1)} %bitcast.25, bf16[1,64,2048]{2,1,0:T(8,128)(2,1)S(1)} %bitcast.26, ...), custom_call_target="tpu_custom_call" | custom-call | tf_op jit(solution)/shard_map/pallas_call | solution.py:476

commit v3 on v2

--- a/solution.py
+++ b/solution.py
@@ -120,7 +120,7 @@
     wg_hbm, wu_hbm, wd_hbm,
     fwd_ref, bwd_ref, gate_grad_ref, wg, wu, wd,
     arrived_ref, prev_ref, cots_ref, next_ref, row_ref, part_ref, arriving,
-    gates_ref, products_ref, returned_ref, weight_ref, sums,
+    dense_ref, gates_ref, products_ref, returned_ref, weight_ref, sums,
     pre_gate, pre_up, d_gate, d_up, gated, hidden_ref,
     shift_send, shift_recv, gate_send, gate_recv, product_send, product_recv,
     gather_send, gather_recv, reduce_send, reduce_recv, weight_sem,
@@ -129,7 +129,6 @@
     half = ring.half
     tokens, width = stash_ref.shape
     local, _, units = wg.shape
-    experts = local * owners
     chunk = width // CHUNKS
     loads = [
         pltpu.make_async_copy(h, v, weight_sem.at[i])
@@ -146,16 +145,20 @@
             values = source[rows, :].astype(F32)
             target[0, rows, :] = (values * scale_of(values) * gain_ref[...].astype(F32)).astype(BF16)
 
+    def padded(rows):
+        rest = jnp.zeros((dense_ref.shape[1] - len(rows), tokens), F32)
+        return jnp.concatenate(rows + [rest], axis=0).astype(BF16)
+
     def dense_gates():
-        lane = lax.broadcasted_iota(jnp.int32, (LANES, tokens), 0)
-        total = jnp.zeros((LANES, tokens), F32)
-        for base, routes, gates in (
-            (0, routes_next_ref, choice_next_ref), (experts, routes_prev_ref, choice_prev_ref)
-        ):
-            names, values = routes[...] + base, gates[...].astype(F32)
-            for k in range(names.shape[0]):
-                total += jnp.where(names[k : k + 1] == lane, values[k : k + 1], 0.0)
-        gates_ref[0] = dot(eye(tokens), total.astype(BF16), 1, 1).astype(BF16)
+        for r in range(owners):
+            first = ring.device(r)[1] * local
+            rows = []
+            for routes, gates in ((routes_next_ref, choice_next_ref), (routes_prev_ref, choice_prev_ref)):
+                for j in range(local):
+                    hit = jnp.where(routes[...] == first + j, gates[...].astype(F32), 0.0)
+                    rows.append(jnp.sum(hit, axis=0, keepdims=True))
+            dense_ref[ring.slot(r)] = padded(rows)
+        gates_ref[0] = dense_ref[0]
 
     buffers, parts = (prev_ref, cots_ref, next_ref), (row_ref, part_ref)
     ways = ((0, 1), (1, -1))
@@ -220,13 +223,16 @@
             + arriving[t, 1, half - 1, rows, :].astype(F32)
         )
 
-    def weights_of(base):
-        rows = flat(gates_ref).astype(F32)
-        lane = lax.broadcasted_iota(jnp.int32, rows.shape, 1)
-        for j in range(local):
-            index = base + ring.me * local + j
-            column = jnp.sum(jnp.where(lane == index, rows, 0.0), axis=1, keepdims=True)
-            weight_ref[base // experts, j] = jnp.broadcast_to(column, rows.shape)
+    def spread_weights():
+        diagonal, ones = eye(tokens), jnp.ones((tokens, LANES), BF16)
+
+        @pl.loop(0, owners)
+        def _(b):
+            held = gates_ref[b]
+            for m in range(2):
+                for j in range(local):
+                    row = held[m * local + j : m * local + j + 1]
+                    weight_ref[m, j, span(b, tokens), :] = dot(diagonal * row, ones, 1, 0)
 
     tile, wide = tile_of(units), tile_of(width)
     inner = units // tile
@@ -296,36 +302,39 @@
         j, rows = n // deep, span(n % deep, tile)
         wd[j, rows, :] = dot(gated[j, :, rows], flat(cots_ref), 0, 0).astype(BF16)
 
-    def small(source, target, sends, receives, own):
+    def small(source, target, sends, receives):
         return [
             send(
-                source.at[0 if own else ring.slot(r)], target.at[ring.slot(-r)],
+                source.at[ring.slot(r)], target.at[ring.slot(-r)],
                 sends.at[r - 1], receives.at[r - 1], ring.device(r),
             )
             for r in range(1, owners)
         ]
 
     def return_products():
-        lane = lax.broadcasted_iota(jnp.int32, sums.shape[1:], 1)
-        total = jnp.zeros(sums.shape[1:], F32)
-        for j in range(local):
-            column = jnp.sum(sums[j], axis=1, keepdims=True)
-            total = jnp.where(lane == ring.me * local + j, column, total)
-        products_ref[...] = total.astype(BF16).reshape(products_ref.shape)
-        go(small(products_ref, returned_ref, product_send, product_recv, False))
+        ones = jnp.ones((dense_ref.shape[1], LANES), F32)
+
+        @pl.loop(0, owners)
+        def _(b):
+            products_ref[b] = padded([
+                lax.dot_general(
+                    ones, sums[j, span(b, tokens), :], (((1,), (1,)), ((), ())),
+                    precision=lax.Precision.HIGHEST, preferred_element_type=F32,
+                )[:1]
+                for j in range(local)
+            ])
+
+        go(small(products_ref, returned_ref, product_send, product_recv))
         returned_ref[0] = products_ref[0]
 
     def backward():
-        come(small(products_ref, returned_ref, product_send, product_recv, False))
-        by_expert = jnp.sum(returned_ref[...].astype(F32), axis=0).astype(BF16)
-        turned = dot(eye(LANES), by_expert, 1, 1)
-        name = lax.broadcasted_iota(jnp.int32, turned.shape, 0)
-        names = routes_prev_ref[...]
-        picks = [
-            jnp.sum(jnp.where(names[k : k + 1] == name, turned, 0.0), axis=0, keepdims=True)
-            for k in range(names.shape[0])
-        ]
-        gate_grad_ref[...] = jnp.concatenate(picks, axis=0).astype(BF16)
+        come(small(products_ref, returned_ref, product_send, product_recv))
+        total = jnp.zeros(gate_grad_ref.shape, F32)
+        for r in range(owners):
+            first, block = ring.device(r)[1] * local, returned_ref[ring.slot(r)].astype(F32)
+            for j in range(local):
+                total += jnp.where(routes_prev_ref[...] == first + j, block[j : j + 1], 0.0)
+        gate_grad_ref[...] = total.astype(BF16)
         for c in range(CHUNKS):
             come(reduce(ROW, c, half - 1))
 
@@ -355,12 +364,12 @@
     both = range(CHUNKS)
 
     normalize(stash_ref, prev_ref)
-    dense_gates()
     met()
     cot_shift.start()
     for c in both:
         pass_on(PREV, c, 0)()
-    gate_copies = small(gates_ref, gates_ref, gate_send, gate_recv, True)
+    dense_gates()
+    gate_copies = small(dense_ref, gates_ref, gate_send, gate_recv)
     go(gate_copies)
     sums[...] = jnp.zeros(sums.shape, F32)
     cot_shift.wait()
@@ -378,8 +387,7 @@
     for action in cots[:CHUNKS] + nexts[:1]:
         action()
     come(gate_copies)
-    for base in (0, experts):
-        weights_of(base)
+    spread_weights()
     for copy in loads:
         copy.wait()
     for c in both:
@@ -415,7 +423,7 @@
             for copies in [gather(t, c, k) for t in range(3)] + [reduce(t, c, k) for t in range(2)]:
                 for copy in copies:
                     copy.wait_send()
-    act_products = small(products_ref, returned_ref, product_send, product_recv, False)
+    act_products = small(products_ref, returned_ref, product_send, product_recv)
     for copy in gate_copies + act_products:
         copy.wait_send()
 
@@ -427,7 +435,7 @@
     every = pltpu.VMEM((owners, tokens, width), BF16)
     inner = (local, owners * tokens, units)
     lanes = (local, owners * tokens, LANES)
-    small = pltpu.VMEM((owners, tokens, LANES), BF16)
+    small = pltpu.VMEM((owners, -(-2 * local // 8) * 8, tokens), BF16)
     peers = pltpu.SemaphoreType.DMA((owners - 1,))
     held = sum(w.size for w in weights) * jnp.dtype(BF16).itemsize
     return pl.pallas_call(
@@ -443,7 +451,7 @@
         scratch_shapes=[pltpu.VMEM((tokens, width), BF16)]
         + [every] * 5
         + [pltpu.VMEM((2, 2, half, tokens, width), BF16)]
-        + [small] * 3
+        + [small] * 4
         + [pltpu.VMEM((2,) + lanes, F32), pltpu.VMEM(lanes, F32)]
         + [pltpu.VMEM(inner, F32)] * 2
         + [pltpu.VMEM(inner, BF16)] * 4

time: 125 us -> 123 us (0.984)
  Pallas kernels: 124 us -> 122 us
    pallas_call x1, Pallas kernels: 117 us -> 115 us  [tick_call(): pl.pallas_call(functools.partial(tick_kernel, sections, owners), out_shap...]
where the time goes in v3:
time: 123 us; the launch traced here: 122 us
  Pallas kernels  122 us (99%)
    pallas_call x1, Pallas kernels, tick_call(): pl.pallas_call(functools.partial(tick_kernel, sections, owners), out_shap...  115 us
    pallas_call x1, Pallas kernels, store(): pl.pallas_call(functools.partial(store_kernel, count), out_shape=tuple((j...  6.86 us

profile of v3, /device:TPU:0, one launch (start us, length us, event | category | flops | bytes accessed | tf_op | source)
XLA Modules:
  0.0 122.5 jit_solution(7364496804281774672)
XLA Ops:
  0.6 115.0 %shard_map.154 = (bf16[64,2048]{1,0:T(8,128)(2,1)S(1)}, bf16[64,2048]{1,0:T(8,128)(2,1)S(1)}, bf16[8,64]{1,0:T(8,128)(2,1)S(1)}, bf16[2,2048,768]{2,1,0:T(8,128)...) custom-call(bf16[64,2048]{1,0:T(8,128)(2,1)} %bitcast.31, bf16[64,2048]{1,0:T(8,128)(2,1)} %bitcast.32, ...), custom_call_target="tpu_custom_call" | custom-call | tf_op jit(solution)/shard_map/pallas_call | solution.py:441
  115.6 6.9 %shard_map.155 = (bf16[1,64,2048]{2,1,0:T(8,128)(2,1)}, bf16[1,64,2048]{2,1,0:T(8,128)(2,1)}, bf16[1,8,64]{2,1,0:T(8,128)(2,1)}, bf16[2,2048,768]{2,1,0:T(8,128)...) custom-call(bf16[1,64,2048]{2,1,0:T(8,128)(2,1)S(1)} %bitcast.25, bf16[1,64,2048]{2,1,0:T(8,128)(2,1)S(1)} %bitcast.26, ...), custom_call_target="tpu_custom_call" | custom-call | tf_op jit(solution)/shard_map/pallas_call | solution.py:484
